TPU v7x, 128 devices: a whole 4x4x4 slice. The times are simulated.
128 devices in a mesh: seq: 4 (over z_lo, core), vocab: 32 (over y, x, z_hi).
Axes of the slice: x: 4, y: 4, z: 4 (z_hi: 2, z_lo: 2; z = z_hi * 2 + z_lo), core: 2. Of those that a mesh axis runs over, the one named last changes fastest.
Arguments:
- hidden: bfloat16 [512, 8192], P('seq'), may hold values from -6 to 6
- steer: float32 [8192], replicated, may hold values from -4 to 4
- tangent: float32 [8192], replicated, may hold values from -6 to 6
- gain: float32 [8192], replicated, may hold values from 0.5 to 1.5
- head: bfloat16 [8192, 77824], P('seq', 'vocab'), may hold values from -0.198873782 to 0.198873782
- target: bfloat16 [512, 77824], P('seq', 'vocab'), may hold values from 0.099609375 to 10
Outputs:
- gradient: float32 [512, 8192], P('vocab', 'seq')
- curvature: float32 [512, 8192], P('vocab', 'seq')
All inputs are finite; a program needn't handle non-finite values.
Results may differ from a plain program's by a relative error of at most 0.0082.
Values may be sent and summed in bfloat16 or wider, within the bound.
A program may use at most 128 MiB of HBM per device.

v0:
```python
import jax
import jax.numpy as jnp
from jax import lax
from jax.sharding import PartitionSpec as P

EPSILON = 1e-06


def norm_back(inputs, radius, denominator, gain_part, upstream_grad, upstream_ggn, feature_count):
    scaled_grad = gain_part * upstream_grad
    scaled_ggn = gain_part * upstream_ggn
    dot_grad, dot_ggn = lax.psum(
        (jnp.sum(inputs * scaled_grad, axis=1), jnp.sum(inputs * scaled_ggn, axis=1)), "seq"
    )
    result_grad = (
        scaled_grad - inputs * (dot_grad / feature_count / denominator)[:, None]
    ) / radius[:, None]
    result_ggn = (scaled_ggn - inputs * (dot_ggn / feature_count / denominator)[:, None]) / radius[
        :, None
    ]
    return (result_grad, result_ggn)


def body(hidden, steer, tangent, gain, head, target):
    seq_index = lax.axis_index("seq")
    feature_count = hidden.shape[1]
    slice_width = head.shape[0]
    vocab_width = head.shape[1]
    relaid = lax.all_to_all(hidden, "seq", split_axis=1, concat_axis=0, tiled=True)
    offset = seq_index * slice_width
    steer_part = lax.dynamic_slice_in_dim(steer, offset, slice_width)
    tangent_part = lax.dynamic_slice_in_dim(tangent, offset, slice_width)
    gain_part = lax.dynamic_slice_in_dim(gain, offset, slice_width)
    inputs = relaid.astype(jnp.float32) + steer_part
    sum_squares, sum_tangent = lax.psum(
        (jnp.sum(inputs * inputs, axis=1), jnp.sum(inputs * tangent_part, axis=1)), "seq"
    )
    denominator = sum_squares / feature_count + EPSILON
    radius = jnp.sqrt(denominator)
    tangent_dot = sum_tangent / feature_count
    normed = (gain_part * inputs / radius[:, None]).astype(jnp.bfloat16)
    tangent_normed = (
        gain_part * (tangent_part - inputs * (tangent_dot / denominator)[:, None]) / radius[:, None]
    ).astype(jnp.bfloat16)
    both_logits = lax.psum_scatter(
        jnp.concatenate(
            [
                jnp.dot(normed, head, preferred_element_type=jnp.float32),
                jnp.dot(tangent_normed, head, preferred_element_type=jnp.float32),
            ],
            axis=1,
        ),
        "seq",
        scatter_dimension=0,
        tiled=True,
    )
    logits = both_logits[:, :vocab_width]
    dlogits = both_logits[:, vocab_width:]
    weights = target.astype(jnp.float32)
    local_peak = jnp.max(logits, axis=1)
    row_peak = lax.pmax(local_peak, "vocab")
    exponent = jnp.exp(logits - row_peak[:, None])
    row_total, shift_total, weight_total = lax.psum(
        (jnp.sum(exponent, axis=1), jnp.sum(exponent * dlogits, axis=1), jnp.sum(weights, axis=1)),
        "vocab",
    )
    softmax_probs = exponent / row_total[:, None]
    mean_shift = shift_total / row_total
    target_probs = weights / weight_total[:, None]
    cot_grad = (softmax_probs - target_probs).astype(jnp.bfloat16)
    cot_ggn = (softmax_probs * (dlogits - mean_shift[:, None])).astype(jnp.bfloat16)
    cotangent = jnp.concatenate([cot_grad, cot_ggn], axis=1)
    gathered = lax.all_gather(cotangent, "seq", axis=0, tiled=True)
    dims = (((1,), (1,)), ((), ()))
    share_rows = gathered.shape[0] // lax.axis_size("vocab")
    start_row = lax.axis_index("vocab") * share_rows
    first_part = lax.dot_general(
        gathered[:, :vocab_width], head, dims, preferred_element_type=jnp.float32
    )
    second_part = lax.dot_general(
        gathered[:, vocab_width:], head, dims, preferred_element_type=jnp.float32
    )
    summed = lax.psum(jnp.concatenate([first_part, second_part], axis=1), "vocab")
    mine = lax.dynamic_slice_in_dim(summed, start_row, share_rows, 0)
    inputs_rows = lax.dynamic_slice_in_dim(inputs, start_row, share_rows, 0)
    radius_rows = lax.dynamic_slice_in_dim(radius, start_row, share_rows, 0)
    denominator_rows = lax.dynamic_slice_in_dim(denominator, start_row, share_rows, 0)
    grad_part, ggn_part = norm_back(
        inputs_rows,
        radius_rows,
        denominator_rows,
        gain_part,
        mine[:, :slice_width],
        mine[:, slice_width:],
        feature_count,
    )
    return (grad_part, ggn_part)


def solution(mesh):
    return jax.shard_map(
        body,
        mesh=mesh,
        in_specs=(P("seq", None), P(), P(), P(), P("seq", "vocab"), P("seq", "vocab")),
        out_specs=(P("vocab", "seq"), P("vocab", "seq")),
        check_vma=False,
    )
```

profile of v0, /device:TPU:0, one launch (start us, length us, event | category | flops | bytes accessed | tf_op | source)
XLA Modules:
  0.0 843.9 jit_solution(12169616497567046853)
XLA Ops:
  7.2 3.2 copy.12
  10.4 3.6 all-to-all-start
  14.0 0.0 reduce-scatter.2.cloned.1.call-start
  14.0 0.7 dynamic_slice.21
  14.7 0.7 dynamic_slice.22
  15.4 0.7 dynamic_slice.23
  16.1 23.5 %all-to-all-done = bf16[128,4,2048]{2,0,1:T(8,128)(2,1)S(1)} async-done(((bf16[128,4,2048]{2,0,1:T(8,128)(2,1)}), bf16[128,4,2048]{2,0,1:T(8,128)(2,1)S(1)}, u32[]{:S(2)}, u32[]{:S(2)}) %all-to-all-start) | async-done | bytes 2097184 | tf_op jit(solution)/shard_map/all_to_all | solution.py:29
  39.6 0.9 multiply_reduce_fusion.1
  40.5 5.8 all-reduce.2
  46.3 0.0 slice-start
  46.3 0.6 bitcast_add_fusion
  46.9 0.0 copy-start.1
  46.9 0.0 slice-start.1
  46.9 0.0 slice-start.2
  46.9 10.6 %fusion.5 = f32[512,2432]{1,0:T(8,128)S(1)} fusion(bf16[2048,2432]{1,0:T(8,128)(2,1)} %param.10, f32[512,2048]{1,0:T(8,128)S(1)} %bitcast_add_fusion, f32[512]{0:T(512)S(1)} %get-tuple-element.22, f32[2048]{0:T(1024)S(1)} %dynamic_slice.21), kind=kOutput, calls=%fused_computation.12 | convolution fusion | flops 5103419392 | bytes 19146752 | tf_op jit(solution)/shard_map/dot_general | solution.py:48
  57.5 0.0 copy-done.1
  57.5 0.0 slice-done
  57.5 0.0 slice-done.1
  57.5 0.0 slice-done.2
  57.5 7.6 fusion.4
  65.1 6.9 pad_maximum_fusion
  72.0 0.0 reduce-scatter.2.cloned.1.call-update
  72.0 0.0 all-gather.2.cloned.1.call-start
  72.1 1.0 copy-done.2
  73.1 0.2 convert_reduce_fusion
  73.3 93.0 %reduce-scatter.2.cloned.1.call-done = f32[128,4864]{1,0:T(8,128)} async-done(((f32[512,4864]{1,0:T(8,128)}), f32[128,4864]{1,0:T(8,128)}) %reduce-scatter.2.cloned.1.call-update) | async-done | bytes 2490384 | tf_op jit(solution)/shard_map/reduce_scatter | solution.py:45
  166.3 0.0 copy-start
  166.3 1.6 slice_reduce_fusion
  167.9 96.0 %pmax.7 = f32[128]{0:T(128)S(1)} all-reduce(f32[128]{0:T(128)S(1)} %slice_reduce_fusion), channel_id=1, replica_groups=mesh['seq'=4,'vocab'=32] {'vocab'}, use_global_device_ids=true, to_apply=%region_6.0 | all-reduce | flops 128 | bytes 1024 | tf_op jit(solution)/shard_map/pmax | solution.py:61
  263.9 2.1 fusion.15
  265.9 88.9 %all-reduce = (f32[128]{0:T(128)S(1)}, f32[128]{0:T(128)S(1)}, f32[128]{0:T(128)S(1)}) all-reduce(f32[128]{0:T(128)S(1)} %get-tuple-element.5, f32[128]{0:T(128)S(1)} %get-tuple-element.4, f32[128]{0:T(128)S(1)} %convert_reduce_fusion), channel_id=1, replica_groups=mesh['seq'=4,'vocab'=32] {'vocab'}, use_global_device_ids=true, to_apply=%region_12.0 | all-reduce | flops 384 | bytes 3072 | tf_op jit(solution)/shard_map/psum | solution.py:63
  354.8 0.0 copy-done
  354.8 0.5 fusion.13
  355.3 1.1 pad_maximum_fusion.2
  356.5 0.0 all-gather.2.cloned.1.call-update
  356.5 0.2 all-reduce.5.cloned.1.call-start
  356.7 49.0 %all-gather.2.cloned.1.call-done = bf16[512,4864]{1,0:T(8,128)(2,1)} async-done(((bf16[128,4864]{1,0:T(8,128)(2,1)}), bf16[512,4864]{1,0:T(8,128)(2,1)}) %all-gather.2.cloned.1.call-update) | async-done | bytes 4980752 | tf_op jit(solution)/shard_map/all_gather | solution.py:73
  405.7 9.2 %fusion = f32[512,2048]{1,0:T(8,128)S(1)} fusion(bf16[2048,2432]{1,0:T(8,128)(2,1)} %param.10, bf16[512,4864]{1,0:T(8,128)(2,1)} %all-gather.2.cloned.1.call-done), kind=kOutput, calls=%fused_computation.7 | convolution fusion | flops 5100273664 | bytes 16646144 | tf_op jit(solution)/shard_map/dot_general | solution.py:80
  414.9 0.0 copy-done.3
  414.9 8.2 fusion.2
  423.1 3.8 pad_maximum_fusion.1
  426.9 0.0 all-reduce.5.cloned.1.call-update
  426.9 0.1 dynamic_slice.27
  427.0 401.5 %all-reduce.5.cloned.1.call-done = f32[512,4096]{1,0:T(8,128)} async-done(((f32[512,4096]{1,0:T(8,128)}), f32[512,4096]{1,0:T(8,128)}) %all-reduce.5.cloned.1.call-update) | async-done | bytes 8388624 | tf_op jit(solution)/shard_map/psum | solution.py:83
  828.5 1.2 multiply_reduce_fusion.3
  829.7 5.8 all-reduce.1
  835.4 0.1 multiply_divide_fusion.1
  835.5 1.8 subtract_divide_fusion
  (5 shorter events, 0.0 us)
Async XLA Ops:
  10.4 29.2 %all-to-all-start = ((bf16[128,4,2048]{2,0,1:T(8,128)(2,1)}), bf16[128,4,2048]{2,0,1:T(8,128)(2,1)S(1)}, u32[]{:S(2)}, u32[]{:S(2)}) async-start(bf16[128,4,2048]{2,0,1:T(8,128)(2,1)} %bitcast.18), calls=%async_computation | async-start | bytes 4194304 | tf_op jit(solution)/shard_map/all_to_all | solution.py:29
  14.0 152.3 %reduce-scatter.2.cloned.1.call-start = ((), (), s32[]{:S(2)}) async-start(), calls=%async_computation.2 | async-start | bytes 12451840 | tf_op jit(solution)/shard_map/reduce_scatter | solution.py:45
  46.3 11.2 %slice-start = ((s8[9961472]{0:T(1024)(128)(4,1)}), s8[4194304]{0:T(1024)(128)(4,1)S(1)}, s32[]{:S(2)}) async-start(s8[9961472]{0:T(1024)(128)(4,1)} %bitcast.22), calls=%async_computation.5 | async-start | bytes 8388608
  46.9 10.6 %copy-start.1 = (f32[512,2048]{1,0:T(8,128)}, f32[512,2048]{1,0:T(8,128)S(1)}, u32[]{:S(2)}) copy-start(f32[512,2048]{1,0:T(8,128)S(1)} %bitcast_add_fusion) | copy-start | bytes 12582916
  46.9 10.6 %slice-start.1 = ((s8[9961472]{0:T(1024)(128)(4,1)}), s8[4194304]{0:T(1024)(128)(4,1)S(1)}, s32[]{:S(2)}) async-start(s8[9961472]{0:T(1024)(128)(4,1)} %bitcast.22), calls=%async_computation.6 | async-start | bytes 8388608
  46.9 10.6 %slice-start.2 = ((s8[9961472]{0:T(1024)(128)(4,1)}), s8[1572864]{0:T(1024)(128)(4,1)S(1)}, s32[]{:S(2)}) async-start(s8[9961472]{0:T(1024)(128)(4,1)} %bitcast.22), calls=%async_computation.7 | async-start | bytes 3145728
  72.0 1.1 copy-start.2
  72.0 333.7 %all-gather.2.cloned.1.call-start = ((), (), s32[]{:S(2)}) async-start(), calls=%async_computation.3 | async-start | bytes 6225920 | tf_op jit(solution)/shard_map/all_gather | solution.py:73
  166.3 188.5 %copy-start = (f32[128,4864]{1,0:T(8,128)S(1)}, f32[128,4864]{1,0:T(8,128)}, u32[]{:S(2)}) copy-start(f32[128,4864]{1,0:T(8,128)} %reduce-scatter.2.cloned.1.call-done) | copy-start | bytes 7471108
  356.5 472.0 %all-reduce.5.cloned.1.call-start = ((), (), s32[]{:S(2)}) async-start(), calls=%async_computation.4 | async-start | bytes 16777216 | tf_op jit(solution)/shard_map/psum | solution.py:83
  405.7 9.2 %copy-start.3 = (bf16[512,4864]{1,0:T(8,128)(2,1)S(1)}, bf16[512,4864]{1,0:T(8,128)(2,1)}, u32[]{:S(2)}) copy-start(bf16[512,4864]{1,0:T(8,128)(2,1)} %all-gather.2.cloned.1.call-done) | copy-start | bytes 14942212
Sparse Core Ops, SparseCore 0:
  72.2 94.0 reduce-scatter.1
  356.6 49.0 all-gather.1
  427.0 401.4 all-reduce.4
where the time goes:
time: 845 us; the launch traced here: 844 us
  waiting for transfers between devices  567 us (67%)
  blocking collectives  196 us (23%)
  matrix products  35.5 us (4%)
  other arithmetic  20.7 us (2%)
  between operations  13.9 us (2%)
    psum x1, waiting for transfers between devices, body(): lax.psum(jnp.concatenate([first_part, second_part], axis=1), 'vocab')  402 us
    pmax x1, blocking collectives, body(): row_peak = lax.pmax(local_peak, 'vocab')  96 us
    reduce_scatter x1, waiting for transfers between devices, body(): lax.psum_scatter(jnp.concatenate([jnp.dot(normed, head, preferred_element...  93 us
    psum x1, blocking collectives, body(): lax.psum((jnp.sum(exponent, axis=1), jnp.sum(exponent * dlogits, axis=1),...  88.9 us
    all_gather x1, waiting for transfers between devices, body(): gathered = lax.all_gather(cotangent, 'seq', axis=0, tiled=True)  49 us
    all_to_all x1, waiting for transfers between devices, body(): lax.all_to_all(hidden, 'seq', split_axis=1, concat_axis=0, tiled=True)  23.5 us
  transfers between devices with their start and end apart: 4, of which 4 were waited for; matrix products, arithmetic and copies ran while one was open for 0% of the time, Pallas kernels for 0%

commit v1 on v0

v1 whole, which is shorter than its diff:
```python
import jax
import jax.numpy as jnp
from jax import lax
from jax.experimental import pallas as pl
from jax.experimental.pallas import tpu as pltpu
from jax.sharding import PartitionSpec as P

EPSILON = 1e-06
MESH = pl.DeviceIdType.MESH
F32 = jnp.float32
BF16 = jnp.bfloat16
NT = (((1,), (1,)), ((), ()))
ROWS = 16
KNEE = 8.0
POWER = 32
SHIFT = 126.0 / POWER


def encode(value):
    code = (1.0 + jnp.abs(value) * (1.0 / KNEE)) * (2.0**-SHIFT)
    for _ in range(5):
        code = code * code
    return jnp.where(value < 0, -code, code).astype(BF16)


def decode(code):
    code = code.astype(F32)
    root = jnp.exp2(jnp.log2(jnp.abs(code)) * (1.0 / POWER) + SHIFT)
    size = (root - 1.0) * KNEE
    return jnp.where(code < 0, -size, size)


def lanes(columns):
    rows = columns[0].shape[0]
    lane = lax.broadcasted_iota(jnp.int32, (rows, 128), 1)
    out = jnp.zeros((rows, 128), F32)
    for place, column in enumerate(columns):
        out = jnp.where(lane == place, column, out)
    return out


def kernel(
    hidden, head_hbm, target, steer, tangent, gain,
    out_grad, out_ggn,
    hfull, hid, stats_in, sq, head, nrm_loc, nrm_rem, upart, uvec, part, psib, code_out, code_in, tgt,
    e_ref, f_ref, gt, ge, gf, norm_col, st_col, st_row, st_in, fin_row, fin_col,
    sb, ropp, rraw, racc, s2, r2, t2, s3, r3,
    loc_sem, hs_s, hs_r, ss_s, ss_r, us_s, us_r, ts_s, ts_r, tf_s, tf_r, ps_s, ps_r, cs_s, cs_r, cf_s, cf_r,
    xs_s, xs_r, a_s, a_r, b_s, b_r, z_s, z_r,
):
    s = lax.axis_index("seq")
    v = lax.axis_index("vocab")
    zl, c = s // 2, s % 2
    y, x, zh = v // 8, (v // 2) % 4, v % 2
    depth = 2048
    width = 2432
    full = 8192
    sib = {"seq": 2 * zl + 1 - c, "vocab": v}
    flip = {"seq": s, "vocab": v + 1 - 2 * zh}

    def pair(core):
        return {"seq": 2 * (1 - zl) + core, "vocab": v}

    def zo(core):
        return {"seq": 2 * (1 - zl) + core, "vocab": v + 1 - 2 * zh}

    def xn(k):
        return {"seq": s, "vocab": y * 8 + ((x + k) % 4) * 2 + zh}

    def yn(k):
        return {"seq": s, "vocab": ((y + k) % 4) * 8 + x * 2 + zh}

    def rc(src, dst, ssem, rsem, dev):
        return pltpu.make_async_remote_copy(
            src_ref=src, dst_ref=dst, send_sem=ssem, recv_sem=rsem, device_id=dev, device_id_type=MESH
        )

    sends = []

    def go(*args):
        copy = rc(*args)
        copy.start()
        sends.append(copy)

    load_head = pltpu.make_async_copy(head_hbm, head, loc_sem.at[0])
    load_hfull = pltpu.make_async_copy(hidden, hfull, loc_sem.at[1])
    my_cols = pl.ds(pl.multiple_of(s * depth, depth), depth)
    load_tgt = pltpu.make_async_copy(target, tgt.at[c], loc_sem.at[2])
    load_own = pltpu.make_async_copy(hidden.at[:, my_cols], hid.at[c], loc_sem.at[3])
    load_hfull.start()
    load_own.start()
    load_head.start()
    load_tgt.start()

    barrier = pltpu.get_barrier_semaphore()
    peers = [sib, pair(0), pair(1), zo(0), zo(1), flip] + [xn(k) for k in (1, 2, 3)] + [yn(k) for k in (1, 2, 3)]
    for peer in peers:
        pl.semaphore_signal(barrier, inc=1, device_id=peer, device_id_type=MESH)
    pl.semaphore_wait(barrier, len(peers))

    def cols_of(seq):
        return pl.ds(pl.multiple_of(seq * depth, depth), depth)

    go(hidden.at[:, cols_of(2 * zl + 1 - c)], hid.at[c], hs_s.at[0], hs_r.at[c], sib)
    for core in range(2):
        go(hidden.at[:, cols_of(2 * (1 - zl) + core)], hid.at[2 + c], hs_s.at[1 + core], hs_r.at[2 + c], zo(core))
    go(target, tgt.at[c], ts_s.at[0], ts_r.at[c], sib)

    load_hfull.wait()

    def sums(i, carry):
        rows = pl.ds(pl.multiple_of(i * ROWS, ROWS), ROWS)
        squares = jnp.zeros((ROWS, 1), F32)
        dots = jnp.zeros((ROWS, 1), F32)
        for q in range(8):
            cols = pl.ds(q * 1024, 1024)
            inputs = hfull[rows, cols].astype(F32) + steer[:, cols]
            squares += jnp.sum(inputs * inputs, axis=1, keepdims=True)
            dots += jnp.sum(inputs * tangent[:, cols], axis=1, keepdims=True)
        sq[rows, :] = lanes([squares, dots])
        return carry

    lax.fori_loop(0, 128 // ROWS, sums, 0)
    stats_in[c] = sq[...].T[0:8, :]
    for place, dev in enumerate((sib, pair(0), pair(1))):
        slot = c if place == 0 else 2 + c
        go(stats_in.at[c], stats_in.at[slot], ss_s.at[place], ss_r.at[slot], dev)
    go(target, tgt.at[2 + c], ts_s.at[1], ts_r.at[2 + c], pair(c))

    steer_part = steer[:, my_cols]
    gain_part = gain[:, my_cols]
    other = 1 - c

    def norm_block(p, dest, base):
        sq[...] = jnp.zeros((128, 128), F32)
        sq[0:8, :] = stats_in[p]
        sq[...] = sq[...].T

        def rows_of(i, carry):
            rows = pl.ds(pl.multiple_of(i * ROWS, ROWS), ROWS)
            both = sq[rows, :]
            denominator = both[:, 0:1] / full + EPSILON
            radius = jnp.sqrt(denominator)
            inverse = 1.0 / radius
            norm_col[p, rows, :] = lanes([inverse, both[:, 1:2] / full / denominator, radius])
            inputs = hid[p, rows, :].astype(F32) + steer_part
            dest[pl.ds(pl.multiple_of(i * ROWS + base, ROWS), ROWS), :] = (gain_part * inputs * inverse).astype(BF16)
            return carry

        lax.fori_loop(0, 128 // ROWS, rows_of, 0)

    def recv(dst, ssem, rsem):
        rc(dst, dst, ssem, rsem, sib).wait_recv()

    product = gain_part * tangent[:, my_cols]
    high = product.astype(BF16).astype(F32)
    row = lax.broadcasted_iota(jnp.int32, (16, depth), 0)
    nrm_loc[256:272, :] = jnp.where(row == 0, high, jnp.where(row == 1, product - high, 0.0)).astype(BF16)

    load_own.wait()
    recv(hid.at[other], hs_s.at[0], hs_r.at[other])
    recv(stats_in.at[other], ss_s.at[0], ss_r.at[other])
    norm_block(0, nrm_loc, 0)
    norm_block(1, nrm_loc, 128)
    load_head.wait()

    tiles = [(0, 512), (512, 512), (1024, 512), (1536, 512), (2048, 384)]
    for start, size in tiles:
        got = jnp.dot(nrm_loc[...], head[:, start : start + size], preferred_element_type=F32)
        part[0, :, start : start + size] = got[0:128]
        part[1, :, start : start + size] = got[128:256]
        upart[s, :, start : start + size] = jnp.sum(got[256:272], axis=0, keepdims=True)
    for p in range(2):
        rc(part.at[p], psib.at[p], ps_s.at[p], ps_r.at[p], sib).start()
    for place, dev in enumerate((sib, pair(0), pair(1))):
        go(upart.at[s], upart.at[s], us_s.at[place], us_r.at[s], dev)

    load_tgt.wait()
    recv(tgt.at[other], ts_s.at[0], ts_r.at[other])

    def target_product(p0):
        def tile(n, carry):
            cols = pl.ds(pl.multiple_of(n * 256, 256), 256)
            lhs = tgt[p0 : p0 + 2].reshape(256, width)
            got = lax.dot_general(lhs, head[cols, :], NT, preferred_element_type=F32)
            gt[pl.ds(p0 * 128, 256), cols] = got
            return carry

        lax.fori_loop(0, 8, tile, 0)

    target_product(0)

    def chip_sum(p0):
        for p in (p0, p0 + 1):
            recv(psib.at[p], ps_s.at[p], ps_r.at[p])

            def rows_of(i, carry):
                rows = pl.ds(pl.multiple_of(i * ROWS, ROWS), ROWS)
                part[p, rows, :] = part[p, rows, :] + psib[p, rows, :]
                return carry

            rc(part.at[p], psib.at[p], ps_s.at[p], ps_r.at[p], sib).wait_send()
            lax.fori_loop(0, 128 // ROWS, rows_of, 0)
        half = p0 // 2

        def code_rows(i, carry):
            rows = pl.ds(pl.multiple_of(i * ROWS, ROWS), ROWS)
            code_out[half, rows, :] = encode(part[p0 + c, rows, :])
            return carry

        lax.fori_loop(0, 128 // ROWS, code_rows, 0)
        go(code_out.at[half], code_in.at[2 - p0 + c], cs_s.at[half], cs_r.at[2 - p0 + c], pair(c))

    chip_sum(0)

    recv(tgt.at[2 + c], ts_s.at[1], ts_r.at[2 + c])
    go(tgt.at[2 + c], tgt.at[2 + c], tf_s.at[0], tf_r.at[c], sib)
    recv(tgt.at[2 + other], tf_s.at[0], tf_r.at[other])
    target_product(2)

    for core in range(2):
        recv(hid.at[2 + core], hs_s.at[1], hs_r.at[2 + core])
        recv(stats_in.at[2 + core], ss_s.at[1], ss_r.at[2 + core])
        norm_block(2 + core, nrm_rem, 128 * core)
    for start, size in tiles:
        got = jnp.dot(nrm_rem[...], head[:, start : start + size], preferred_element_type=F32)
        part[2, :, start : start + size] = got[0:128]
        part[3, :, start : start + size] = got[128:256]
    for p in (2, 3):
        rc(part.at[p], psib.at[p], ps_s.at[p], ps_r.at[p], sib).start()
    chip_sum(2)

    recv(upart.at[2 * zl + other], us_s.at[0], us_r.at[2 * zl + other])
    for core in range(2):
        recv(upart.at[2 * (1 - zl) + core], us_s.at[1], us_r.at[2 * (1 - zl) + core])
    uvec[...] = (upart[0] + upart[1]) + (upart[2] + upart[3])

    def softmax_rows(p):
        def rows_of(i, carry):
            rows = pl.ds(pl.multiple_of(i * ROWS, ROWS), ROWS)
            logits = part[p, rows, :] + decode(code_in[p, rows, :])
            part[p, rows, :] = logits
            peak = jnp.max(logits, axis=1, keepdims=True)
            columns = norm_col[p, rows, :]
            inverse, along = columns[:, 0:1], columns[:, 1:2]
            u = uvec[...]
            exponent = jnp.exp(logits - peak)
            dlogits = u * inverse - along * logits
            total = jnp.sum(exponent, axis=1, keepdims=True)
            shift = jnp.sum(exponent * dlogits, axis=1, keepdims=True)
            first = jnp.sum(exponent * logits, axis=1, keepdims=True)
            weights = tgt[p, rows, :].astype(F32)
            weight_total = jnp.sum(weights, axis=1, keepdims=True)
            weight_first = jnp.sum(weights * logits, axis=1, keepdims=True)
            mean = shift / total
            weighted = exponent * (dlogits - mean)
            second = jnp.sum(weighted * logits, axis=1, keepdims=True) + mean * first
            e_ref[p, rows, :] = exponent.astype(BF16)
            f_ref[p, rows, :] = weighted.astype(BF16)
            st_col[rows, :] = lanes([peak, total, shift, first, second, weight_total, weight_first])
            return carry

        lax.fori_loop(0, 128 // ROWS, rows_of, 0)
        st_row[p] = st_col[...].T[0:8, :]

    for p0 in (2, 0):
        recv(code_in.at[p0 + c], cs_s.at[0], cs_r.at[p0 + c])
        go(code_in.at[p0 + c], code_in.at[p0 + c], cf_s.at[p0 // 2], cf_r.at[p0 // 2], sib)
        recv(code_in.at[p0 + other], cf_s.at[p0 // 2], cf_r.at[p0 // 2])
        softmax_rows(p0)
        softmax_rows(p0 + 1)

    def merge(a, b):
        peak = jnp.maximum(a[:, 0:1], b[:, 0:1])
        lane = lax.broadcasted_iota(jnp.int32, (4, 8, 128), 1)
        scale_a = jnp.where(lane < 5, jnp.exp(a[:, 0:1] - peak), 1.0)
        scale_b = jnp.where(lane < 5, jnp.exp(b[:, 0:1] - peak), 1.0)
        return jnp.where(lane == 0, peak, a * scale_a + b * scale_b)

    st_in[7] = st_row[...]
    for stage, hop in enumerate((xn, yn)):
        for k in (1, 2, 3):
            slot = 3 * stage + k - 1
            go(st_in.at[7 + stage], st_in.at[slot], xs_s.at[slot], xs_r.at[slot], hop(k))
        total = st_in[7 + stage]
        for k in (1, 2, 3):
            slot = 3 * stage + k - 1
            recv(st_in.at[slot], xs_s.at[slot], xs_r.at[slot])
            total = merge(total, st_in[slot])
        st_in[8 + stage] = total
    go(st_in.at[9], st_in.at[6], xs_s.at[6], xs_r.at[6], flip)
    recv(st_in.at[6], xs_s.at[6], xs_r.at[6])
    total = merge(st_in[9], st_in[6])
    for p in range(4):
        mine = st_row[p]
        sums_of = total[p]
        factor = jnp.exp(mine[0:1] - sums_of[0:1]) / sums_of[1:2]
        shift = sums_of[2:3] / sums_of[1:2]
        turn = factor * (mine[2:3] / mine[1:2] - shift)
        weight = 1.0 / sums_of[5:6]
        mean_logit = sums_of[3:4] / sums_of[1:2]
        dot_grad = mean_logit - sums_of[6:7] * weight
        dot_ggn = sums_of[4:5] / sums_of[1:2] - shift * mean_logit
        sq[...] = jnp.zeros((128, 128), F32)
        for place, line in enumerate((factor, turn, weight, dot_grad, dot_ggn)):
            sq[place : place + 1, :] = line
        fin_col[p] = sq[...].T

    def ring(o, stage):
        along_x = o == stage
        if along_x:
            return xn(1), xn(3), lambda k: (x + k) % 4
        return yn(1), yn(3), lambda k: (y + k + 2 * zl) % 4

    def stage1(o, n):
        right, left, at = ring(o, 0)
        opp = [
            rc(sb.at[o, n, 0, at(2)], ropp.at[o, n, 0], a_s.at[o, n, 0], a_r.at[o, n, 0], right),
            rc(sb.at[o, n, 1, at(2)], ropp.at[o, n, 1], a_s.at[o, n, 1], a_r.at[o, n, 1], left),
        ]
        raw = [
            rc(sb.at[o, n, 1, at(1)], rraw.at[o, n, 1], a_s.at[o, n, 2], a_r.at[o, n, 2], right),
            rc(sb.at[o, n, 0, at(3)], rraw.at[o, n, 0], a_s.at[o, n, 3], a_r.at[o, n, 3], left),
        ]
        acc = [
            rc(sb.at[o, n, 0, at(1)], racc.at[o, n, 0], a_s.at[o, n, 4], a_r.at[o, n, 4], right),
            rc(sb.at[o, n, 1, at(3)], racc.at[o, n, 1], a_s.at[o, n, 5], a_r.at[o, n, 5], left),
        ]
        return at, opp, raw, acc

    def relay(n):
        for o in range(2):
            at, opp, raw, acc = stage1(o, n)
            for h in range(2):
                opp[h].wait_recv()
                where = at(1) if h == 0 else at(3)
                sb[o, n, h, where] = (sb[o, n, h, where].astype(F32) + ropp[o, n, h].astype(F32)).astype(BF16)
                acc[h].start()

    def chunk(n, carry):
        cols = pl.ds(pl.multiple_of(n * 512, 512), 512)
        block = head[cols, :]
        ge[...] = lax.dot_general(e_ref[...].reshape(512, width), block, NT, preferred_element_type=F32)
        gf[...] = lax.dot_general(f_ref[...].reshape(512, width), block, NT, preferred_element_type=F32)
        for p in range(4):
            for k in range(4):
                rows = pl.ds(p * 128 + k * 32, 32)
                columns = fin_col[p, pl.ds(k * 32, 32), :]
                factor, turn, weight = columns[:, 0:1], columns[:, 1:2], columns[:, 2:3]
                value = ge[rows, :]
                grad = factor * value - weight * gt[rows, cols]
                ggn = factor * gf[rows, :] + turn * value
                for h in range(2):
                    sb[0, n, h, k, pl.ds(p * 32, 32), :] = grad[:, h * 256 : (h + 1) * 256].astype(BF16)
                    sb[1, n, h, p, pl.ds(k * 32, 32), :] = ggn[:, h * 256 : (h + 1) * 256].astype(BF16)
        for o in range(2):
            at, opp, raw, acc = stage1(o, n)
            for copy in opp + raw:
                copy.start()

        @pl.when(n > 0)
        def _():
            relay(n - 1)

        return carry

    lax.fori_loop(0, 4, chunk, 0)
    relay(3)

    for n in range(4):
        for o in range(2):
            at, opp, raw, acc = stage1(o, n)
            for h in range(2):
                raw[1 - h].wait_recv()
                acc[h].wait_recv()
                mine = sb[o, n, h, at(0)].astype(F32) + racc[o, n, h].astype(F32) + rraw[o, n, h].astype(F32)
                first = (n % 2) * 512 + h * 256
                for d in range(4):
                    s2[o, n // 2, d, :, first : first + 256] = mine[d * 32 : (d + 1) * 32].astype(BF16)

    steps = []
    for o in range(2):
        right, left, at = ring(o, 1)
        opp = [
            rc(s2.at[o, 0, at(2)], r2.at[o, 0], b_s.at[o, 0], b_r.at[o, 0], right),
            rc(s2.at[o, 1, at(2)], r2.at[o, 1], b_s.at[o, 1], b_r.at[o, 1], left),
        ]
        raw = [
            rc(s2.at[o, 0, at(3)], r2.at[o, 2], b_s.at[o, 2], b_r.at[o, 2], left),
            rc(s2.at[o, 1, at(1)], r2.at[o, 3], b_s.at[o, 3], b_r.at[o, 3], right),
        ]
        acc = [
            rc(s2.at[o, 0, at(1)], r2.at[o, 4], b_s.at[o, 4], b_r.at[o, 4], right),
            rc(s2.at[o, 1, at(3)], r2.at[o, 5], b_s.at[o, 5], b_r.at[o, 5], left),
        ]
        for copy in opp + raw:
            copy.start()
        steps.append((at, opp, raw, acc))
    for o in range(2):
        at, opp, raw, acc = steps[o]
        for h in range(2):
            opp[h].wait_recv()
            where = at(1) if h == 0 else at(3)
            s2[o, h, where] = (s2[o, h, where].astype(F32) + r2[o, h].astype(F32)).astype(BF16)
            acc[h].start()
    last = []
    for o in range(2):
        at, opp, raw, acc = steps[o]
        for h in range(2):
            raw[h].wait_recv()
            acc[h].wait_recv()
            mine = s2[o, h, at(0)].astype(F32) + r2[o, 2 + h].astype(F32) + r2[o, 4 + h].astype(F32)
            for z in range(2):
                t2[o, z, :, h * 1024 : (h + 1) * 1024] = mine[z * 16 : (z + 1) * 16]
        s3[o] = t2[o, 1 - zh].astype(BF16)
        copy = rc(s3.at[o], r3.at[o], z_s.at[o], z_r.at[o], flip)
        copy.start()
        last.append(copy)

    p_mine = (y + 2 * zl) % 4
    rows = pl.ds(pl.multiple_of(x * 32 + zh * 16, 16), 16)
    inputs = hid[p_mine, rows, :].astype(F32) + steer_part
    inverse = norm_col[p_mine, rows, :][:, 0:1]
    columns = fin_col[p_mine, rows, :]
    for o, out in enumerate((out_grad, out_ggn)):
        last[o].wait_recv()
        back = t2[o, zh] + r3[o].astype(F32)
        slope = columns[:, 3 + o : 4 + o] * inverse * (1.0 / full)
        out[...] = (gain_part * back - inputs * slope) * inverse

    for n in range(4):
        for o in range(2):
            at, opp, raw, acc = stage1(o, n)
            for copy in opp + raw + acc:
                copy.wait_send()
    for at, opp, raw, acc in steps:
        for copy in opp + raw + acc:
            copy.wait_send()
    for copy in last:
        copy.wait_send()
    for copy in sends:
        copy.wait_send()


def body(hidden, steer, tangent, gain, head, target):
    vmem = pltpu.VMEM
    dma = pltpu.SemaphoreType.DMA
    any_spec = pl.BlockSpec(memory_space=pl.ANY)
    vmem_spec = pl.BlockSpec(memory_space=pltpu.VMEM)
    return pl.pallas_call(
        kernel,
        out_shape=[jax.ShapeDtypeStruct((16, 2048), F32)] * 2,
        in_specs=[any_spec] * 3 + [vmem_spec] * 3,
        out_specs=[vmem_spec] * 2,
        scratch_shapes=[
            vmem((128, 8192), BF16),
            vmem((4, 128, 2048), BF16),
            vmem((4, 8, 128), F32),
            vmem((128, 128), F32),
            vmem((2048, 2432), BF16),
            vmem((272, 2048), BF16),
            vmem((256, 2048), BF16),
            vmem((4, 1, 2432), F32),
            vmem((1, 2432), F32),
            vmem((4, 128, 2432), F32),
            vmem((4, 128, 2432), F32),
            vmem((2, 128, 2432), BF16),
            vmem((4, 128, 2432), BF16),
            vmem((4, 128, 2432), BF16),
            vmem((4, 128, 2432), BF16),
            vmem((4, 128, 2432), BF16),
            vmem((512, 2048), F32),
            vmem((512, 512), F32),
            vmem((512, 512), F32),
            vmem((4, 128, 128), F32),
            vmem((128, 128), F32),
            vmem((4, 8, 128), F32),
            vmem((10, 4, 8, 128), F32),
            vmem((8, 128), F32),
            vmem((4, 128, 128), F32),
            vmem((2, 4, 2, 4, 128, 256), BF16),
            vmem((2, 4, 2, 128, 256), BF16),
            vmem((2, 4, 2, 128, 256), BF16),
            vmem((2, 4, 2, 128, 256), BF16),
            vmem((2, 2, 4, 32, 1024), BF16),
            vmem((2, 6, 32, 1024), BF16),
            vmem((2, 2, 16, 2048), F32),
            vmem((2, 16, 2048), BF16),
            vmem((2, 16, 2048), BF16),
            dma((4,)),
            dma((3,)), dma((4,)),
            dma((3,)), dma((4,)),
            dma((3,)), dma((4,)),
            dma((2,)), dma((4,)),
            dma((1,)), dma((2,)),
            dma((4,)), dma((4,)),
            dma((2,)), dma((4,)),
            dma((2,)), dma((2,)),
            dma((7,)), dma((7,)),
            dma((2, 4, 6)), dma((2, 4, 6)),
            dma((2, 6)), dma((2, 6)),
            dma((2,)), dma((2,)),
        ],
        compiler_params=pltpu.CompilerParams(
            collective_id=0, has_side_effects=True, vmem_limit_bytes=66 * 1024 * 1024 - 2 * 1024 * 1024
        ),
    )(hidden, head, target, steer.reshape(1, -1), tangent.reshape(1, -1), gain.reshape(1, -1))


def solution(mesh):
    return jax.shard_map(
        body,
        mesh=mesh,
        in_specs=(P("seq", None), P(), P(), P(), P("seq", "vocab"), P("seq", "vocab")),
        out_specs=(P("vocab", "seq"), P("vocab", "seq")),
        check_vma=False,
    )
```

time: 845 us -> 118 us (0.14)
  waiting for transfers between devices: 567 us -> 0 us
  blocking collectives: 196 us -> 0 us
  Pallas kernels: 0 us -> 114 us
  matrix products: 35.5 us -> 0 us
  other arithmetic: 20.7 us -> 0 us
  between operations: 13.9 us -> 0.64 us
    psum x1 -> x0, waiting for transfers between devices: 402 us -> none  [body(): lax.psum(jnp.concatenate([first_part, second_part], axis=1), 'vocab')]
    pallas_call x0 -> x1, Pallas kernels: none -> 114 us  [body(): pl.pallas_call(kernel, out_shape=[jax.ShapeDtypeStruct((16, 2048), F32)]...]
    psum x3 -> x0, blocking collectives: 100 us -> none  [the longest x1 88.9 us: body(): lax.psum((jnp.sum(exponent, axis=1), jnp.sum(exponent * dlogits, axis=1),...]
    pmax x1 -> x0, blocking collectives: 96 us -> none  [body(): row_peak = lax.pmax(local_peak, 'vocab')]
    reduce_scatter x1 -> x0, waiting for transfers between devices: 93 us -> none  [body(): lax.psum_scatter(jnp.concatenate([jnp.dot(normed, head, preferred_element...]
    all_gather x1 -> x0, waiting for transfers between devices: 49 us -> none  [body(): gathered = lax.all_gather(cotangent, 'seq', axis=0, tiled=True)]
    dot_general x4 -> x0, matrix products: 35.5 us -> none  [the longest x1 10.6 us: body(): jnp.dot(normed, head, preferred_element_type=jnp.float32)]
    all_to_all x1 -> x0, waiting for transfers between devices: 23.5 us -> none  [body(): lax.all_to_all(hidden, 'seq', split_axis=1, concat_axis=0, tiled=True)]
  transfers between devices with their start and end apart: 4 -> 0, of which waited for: 4 -> 0; matrix products, arithmetic and copies ran while one was open for 0% -> 0% of each run, Pallas kernels for 0% -> 0%
where the time goes in v1:
time: 118 us
  Pallas kernels  114 us (97%)
  local copies, waits for them, and re-layouts  3.14 us (3%)
    pallas_call x1, Pallas kernels, body(): pl.pallas_call(kernel, out_shape=[jax.ShapeDtypeStruct((16, 2048), F32)]...  114 us
    unnamed x2, local copies, waits for them, and re-layouts  3.14 us

profile of v1, /device:TPU:0, one launch (start us, length us, event | category | flops | bytes accessed | tf_op | source)
XLA Modules:
  0.0 117.5 jit_solution(13075771284412427154)
XLA Ops:
  0.6 113.7 %shard_map.77 = (f32[16,2048]{1,0:T(8,128)}, f32[16,2048]{1,0:T(8,128)}) custom-call(bf16[128,8192]{1,0:T(8,128)(2,1)} %hidden.1, bf16[2048,2432]{1,0:T(8,128)(2,1)} %head_hbm.1, bf16[128,2432]{1,0:T(8,128)(2,1)} %target.1, f32[1,8192]{1,0:T(1,128)} %bitcast.3, f32[1,8192]{1,0:T(1,128)} %bitcast.4, f32[1,8192]{1,0:T(1,128)} %bitcast.5), custom_call_target="tpu_custom_call" | custom-call | tf_op jit(solution)/shard_map/pallas_call | solution.py:450
  114.4 1.6 %copy.10 = f32[16,2048]{1,0:T(8,128)} copy(f32[16,2048]{1,0:T(8,128)} %get-tuple-element.4) | data formatting | bytes 262144
  115.9 1.6 %copy.11 = f32[16,2048]{1,0:T(8,128)} copy(f32[16,2048]{1,0:T(8,128)} %get-tuple-element.5) | data formatting | bytes 262144

commit v2 on v0

v2 whole, which is shorter than its diff:
```python
import jax
import jax.numpy as jnp
from jax import lax
from jax.experimental import pallas as pl
from jax.experimental.pallas import tpu as pltpu
from jax.sharding import PartitionSpec as P

EPSILON = 1e-06
MESH = pl.DeviceIdType.MESH
F32 = jnp.float32
BF16 = jnp.bfloat16
NT = (((1,), (1,)), ((), ()))
ROWS = 16
KNEE = 8.0
POWER = 32
SHIFT = 126.0 / POWER


def encode(value):
    code = (1.0 + jnp.abs(value) * (1.0 / KNEE)) * (2.0**-SHIFT)
    for _ in range(5):
        code = code * code
    return jnp.where(value < 0, -code, code).astype(BF16)


def decode(code):
    code = code.astype(F32)
    root = jnp.exp2(jnp.log2(jnp.abs(code)) * (1.0 / POWER) + SHIFT)
    size = (root - 1.0) * KNEE
    return jnp.where(code < 0, -size, size)


def lanes(columns):
    rows = columns[0].shape[0]
    lane = lax.broadcasted_iota(jnp.int32, (rows, 128), 1)
    out = jnp.zeros((rows, 128), F32)
    for place, column in enumerate(columns):
        out = jnp.where(lane == place, column, out)
    return out


class Reduce:
    def __init__(self, ring, buffer, landing, send_sem, recv_sem):
        self.ring, self.buffer, self.landing = ring, buffer, landing
        self.send_sem, self.recv_sem = send_sem, recv_sem

    def copies(self, route, n):
        right, left, at = self.ring(route)

        def copy(h, kind, dest, device):
            return pltpu.make_async_remote_copy(
                src_ref=self.buffer.at[route, n, h, dest],
                dst_ref=self.landing.at[route, n, h, kind],
                send_sem=self.send_sem.at[0],
                recv_sem=self.recv_sem.at[n, min(kind, 1)],
                device_id=device,
                device_id_type=MESH,
            )

        opposite = [copy(0, 0, at(2), right), copy(1, 0, at(2), left)]
        raw = [copy(0, 1, at(3), left), copy(1, 1, at(1), right)]
        summed = [copy(0, 2, at(1), right), copy(1, 2, at(3), left)]
        return at, opposite, raw, summed

    def send(self, n):
        for route in range(2):
            _, opposite, raw, _ = self.copies(route, n)
            for copy in opposite + raw:
                copy.start()

    def all_of(self, ref, recv_sem):
        return pltpu.make_async_remote_copy(
            src_ref=ref, dst_ref=ref, send_sem=self.send_sem.at[0], recv_sem=recv_sem,
            device_id=self.ring(0)[0], device_id_type=MESH,
        )

    def relay(self, n):
        self.all_of(self.landing.at[:, n, :, 0], self.recv_sem.at[n, 0]).wait_recv()
        for route in range(2):
            at, _, _, summed = self.copies(route, n)
            for h in range(2):
                where = at(1) if h == 0 else at(3)
                mine = self.buffer[route, n, h, where].astype(F32)
                self.buffer[route, n, h, where] = (mine + self.landing[route, n, h, 0].astype(F32)).astype(BF16)
                summed[h].start()

    def wait(self, n):
        self.all_of(self.landing.at[:, n, :, 1:3], self.recv_sem.at[n, 1]).wait_recv()

    def total(self, route, n, h, o, rows):
        at = self.ring(route)[2]
        out = self.buffer[route, n, h, at(0), o, rows, :].astype(F32)
        return out + self.landing[route, n, h, 1, o, rows, :].astype(F32) + self.landing[route, n, h, 2, o, rows, :].astype(F32)

    def drain(self):
        self.all_of(self.landing, self.recv_sem.at[0, 0]).wait_send()


def kernel(
    hidden, head_hbm, target, steer, tangent, gain,
    out, out_col,
    hfull, hid, stats_in, sq, head, nrm_loc, nrm_rem, upart, uvec, part, psib, code_out, code_in, tgt,
    ef, norm_col, st_col, st_in, fin_col, wide, fin2, fin3,
    sb, r1, s2, r2, t2, s3, r3, gsb, gr1, gs2, gr2, gt2, gs3, gr3,
    loc_sem, hs_s, hs_r, fs_s, fs_r, hr_s, hr_r, ss_s, ss_r, us_s, us_r, ts_s, ts_r, tf_s, tf_r, ps_s, ps_r,
    cs_s, cs_r, cf_s, cf_r, xs_s, xs_r, a_s, a_r, b_s, b_r, z_s, z_r, ga_s, ga_r, gb_s, gb_r, gz_s, gz_r,
):
    s = lax.axis_index("seq")
    v = lax.axis_index("vocab")
    zl, c = s // 2, s % 2
    y, x, zh = v // 8, (v // 2) % 4, v % 2
    depth = 2048
    width = 2432
    full = 8192
    other = 1 - c
    p_mine = (y + 2 * zl) % 4
    sib = {"seq": 2 * zl + 1 - c, "vocab": v}
    flip = {"seq": s, "vocab": v + 1 - 2 * zh}

    def pair(core):
        return {"seq": 2 * (1 - zl) + core, "vocab": v}

    def zo(core):
        return {"seq": 2 * (1 - zl) + core, "vocab": v + 1 - 2 * zh}

    def xn(k):
        return {"seq": s, "vocab": y * 8 + ((x + k) % 4) * 2 + zh}

    def yn(k):
        return {"seq": s, "vocab": ((y + k) % 4) * 8 + x * 2 + zh}

    def ring_of(stage):
        def ring(route):
            if route == stage:
                return xn(1), xn(3), lambda k: (x + k) % 4
            return yn(1), yn(3), lambda k: (y + k + 2 * zl) % 4

        return ring

    def rc(src, dst, ssem, rsem, dev):
        return pltpu.make_async_remote_copy(
            src_ref=src, dst_ref=dst, send_sem=ssem, recv_sem=rsem, device_id=dev, device_id_type=MESH
        )

    sends = []

    def go(*args):
        copy = rc(*args)
        copy.start()
        sends.append(copy)

    def recv(dst, ssem, rsem):
        rc(dst, dst, ssem, rsem, sib).wait_recv()

    def cols_of(seq):
        return pl.ds(pl.multiple_of(seq * depth, depth), depth)

    def sixteen(i):
        return pl.ds(pl.multiple_of(i * ROWS, ROWS), ROWS)

    my_cols = cols_of(s)
    load_head = pltpu.make_async_copy(head_hbm, head, loc_sem.at[0])
    load_hfull = pltpu.make_async_copy(hidden, hfull, loc_sem.at[1])
    load_tgt = pltpu.make_async_copy(target, tgt.at[c], loc_sem.at[2])
    load_own = pltpu.make_async_copy(hidden.at[:, my_cols], hid.at[c], loc_sem.at[3])
    load_tgt.start()
    load_hfull.start()
    load_own.start()

    barrier = pltpu.get_barrier_semaphore()
    peers = [sib, pair(0), pair(1), zo(0), zo(1), flip] + [xn(k) for k in (1, 2, 3)] + [yn(k) for k in (1, 2, 3)]
    for peer in peers:
        pl.semaphore_signal(barrier, inc=1, device_id=peer, device_id_type=MESH)
    pl.semaphore_wait(barrier, len(peers))

    def piece(half, k):
        place = ((x if half == 0 else y) + k) % 4
        return pl.ds(pl.multiple_of(half * 64 + place * 16, 16), 16)

    go(hidden.at[:, cols_of(2 * zl + 1 - c)], hid.at[c], hs_s.at[0], hs_r.at[c], sib)
    for core in range(2):
        for half in range(2):
            rows = piece(half, 0)
            go(
                hidden.at[rows, cols_of(2 * (1 - zl) + core)], hid.at[2 + c, rows, :],
                fs_s.at[core, half], fs_r.at[c, half], zo(core),
            )
    load_tgt.wait()
    go(tgt.at[c], tgt.at[2 + c], ts_s.at[1], ts_r.at[2 + c], pair(c))
    go(tgt.at[c], tgt.at[c], ts_s.at[0], ts_r.at[c], sib)
    load_head.start()

    load_hfull.wait()

    def sums(i, carry):
        rows = sixteen(i)
        squares = jnp.zeros((ROWS, 1), F32)
        dots = jnp.zeros((ROWS, 1), F32)
        for q in range(8):
            cols = pl.ds(q * 1024, 1024)
            inputs = hfull[rows, cols].astype(F32) + steer[:, cols]
            squares += jnp.sum(inputs * inputs, axis=1, keepdims=True)
            dots += jnp.sum(inputs * tangent[:, cols], axis=1, keepdims=True)
        sq[rows, :] = lanes([squares, dots])
        return carry

    lax.fori_loop(0, 128 // ROWS, sums, 0)
    stats_in[c] = sq[...].T[0:8, :]
    for place, dev in enumerate((sib, zo(0), zo(1))):
        slot = c if place == 0 else 2 + c
        go(stats_in.at[c], stats_in.at[slot], ss_s.at[place], ss_r.at[slot], dev)

    def hop(half, k):
        return xn(k) if half == 0 else yn(k)

    def ring_start():
        for core in range(2):
            for half in range(2):
                ref = hid.at[2 + core, piece(half, 0), :]
                recv(ref, fs_s.at[core, half], fs_r.at[core, half])
                for way in range(2):
                    go(ref, ref, hr_s.at[core, half, way], hr_r.at[core, half, way], hop(half, 1 + 2 * way))

    def ring_relay():
        for core in range(2):
            for half in range(2):
                for way in range(2):
                    rows = piece(half, 3 - 2 * way)
                    recv(hid.at[2 + core, rows, :], hr_s.at[core, half, way], hr_r.at[core, half, way])
                    ref = hid.at[2 + core, rows, way * 1024 : (way + 1) * 1024]
                    go(ref, ref, hr_s.at[core, half, 2 + way], hr_r.at[core, half, 2 + way], hop(half, 1 + 2 * way))

    def ring_end(core):
        for half in range(2):
            for way in range(2):
                ref = hid.at[2 + core, piece(half, 2), way * 1024 : (way + 1) * 1024]
                recv(ref, hr_s.at[core, half, 2 + way], hr_r.at[core, half, 2 + way])

    steer_part = steer[:, my_cols]
    gain_part = gain[:, my_cols]

    def norm_block(p, dest, base):
        sq[...] = jnp.zeros((128, 128), F32)
        sq[0:8, :] = stats_in[p]
        sq[...] = sq[...].T

        def rows_of(i, carry):
            rows = sixteen(i)
            both = sq[rows, :]
            denominator = both[:, 0:1] / full + EPSILON
            inverse = 1.0 / jnp.sqrt(denominator)
            norm_col[i % 2, p, sixteen(i // 2), :] = lanes([inverse, both[:, 1:2] / full / denominator])
            inputs = hid[p, rows, :].astype(F32) + steer_part
            dest[pl.ds(pl.multiple_of((i % 2) * 128 + base + (i // 2) * ROWS, ROWS), ROWS), :] = (gain_part * inputs * inverse).astype(BF16)
            return carry

        lax.fori_loop(0, 128 // ROWS, rows_of, 0)

    product = gain_part * tangent[:, my_cols]
    high = product.astype(BF16).astype(F32)
    row = lax.broadcasted_iota(jnp.int32, (16, depth), 0)
    nrm_loc[256:272, :] = jnp.where(row == 0, high, jnp.where(row == 1, product - high, 0.0)).astype(BF16)

    load_own.wait()
    recv(hid.at[other], hs_s.at[0], hs_r.at[other])
    recv(stats_in.at[other], ss_s.at[0], ss_r.at[other])
    norm_block(0, nrm_loc, 0)
    norm_block(1, nrm_loc, 64)
    ring_start()
    load_head.wait()

    tiles = [(0, 512), (512, 512), (1024, 512), (1536, 512), (2048, 384)]

    def send_codes(half, z, t):
        cols = slice(tiles[t][0], tiles[t][0] + tiles[t][1])
        go(
            code_out.at[half, z, :, cols], code_in.at[z, 2 - 2 * half + c, :, cols],
            cs_s.at[half, z, t], cs_r.at[half, z, t], pair(c),
        )

    def forward(half):
        p0 = 2 * half

        def finish(t):
            start, size = tiles[t]
            cols = slice(start, start + size)
            recv(psib.at[:, p0 + c, :, cols], ps_s.at[half, t], ps_r.at[half, t])

            def rows_of(i, carry):
                rows = sixteen(i // 2)
                z = i % 2
                value = part[z, p0 + c, rows, cols] + psib[z, p0 + c, rows, cols]
                psib[z, p0 + c, rows, cols] = value
                code_out[half, z, rows, cols] = encode(value)
                return carry

            lax.fori_loop(0, 128 // ROWS, rows_of, 0)
            send_codes(half, 0, t)

        for t, (start, size) in enumerate(tiles):
            cols = slice(start, start + size)
            lhs = nrm_loc if half == 0 else nrm_rem
            got = jnp.dot(lhs[...], head[:, cols], preferred_element_type=F32)
            for z in range(2):
                for p in range(2):
                    first = z * 128 + p * 64
                    part[z, p0 + p, :, cols] = got[first : first + 64]
            if half == 0:
                upart[s, :, cols] = jnp.sum(got[256:272], axis=0, keepdims=True)
            rc(
                part.at[:, p0 + other, :, cols], psib.at[:, p0 + other, :, cols],
                ps_s.at[half, t], ps_r.at[half, t], sib,
            ).start()
            if t:
                finish(t - 1)
        finish(len(tiles) - 1)

    g1 = Reduce(ring_of(0), gsb, gr1, ga_s, ga_r)
    g2 = Reduce(ring_of(1), gs2, gr2, gb_s, gb_r)
    m1 = Reduce(ring_of(0), sb, r1, a_s, a_r)
    m2 = Reduce(ring_of(1), s2, r2, b_s, b_r)

    def store(buffer, n, o, p, k, value):
        for h in range(2):
            cols = slice(h * 128, (h + 1) * 128)
            buffer[0, n, h, k, o, pl.ds(p * 32, 32), :] = value[0][:, cols].astype(BF16)
            buffer[1, n, h, p, o, pl.ds(k * 32, 32), :] = value[1][:, cols].astype(BF16)

    def target_chunk(p0, n):
        block = head[pl.ds(pl.multiple_of(n * 512, 512), 512), :]
        got = lax.dot_general(tgt[p0 : p0 + 2].reshape(256, width), block, NT, preferred_element_type=F32)
        for p in range(2):
            for k in range(4):
                rows = got[p * 128 + k * 32 : p * 128 + k * 32 + 32]
                store(gsb, n, 0, p0 + p, k, (rows[:, 0:256], rows[:, 256:512]))

    def target_near(n, carry):
        target_chunk(0, n)
        return carry

    def target_far(n, carry):
        target_chunk(2, n)
        g1.send(n)
        return carry

    forward(0)
    for place, dev in enumerate((sib, pair(0), pair(1))):
        go(upart.at[s], upart.at[s], us_s.at[place], us_r.at[s], dev)
    ring_relay()
    recv(tgt.at[other], ts_s.at[0], ts_r.at[other])
    lax.fori_loop(0, 4, target_near, 0)
    for core in range(2):
        ring_end(core)
        recv(stats_in.at[2 + core], ss_s.at[1], ss_r.at[2 + core])
        norm_block(2 + core, nrm_rem, 64 * core)
    forward(1)
    for half in range(2):
        for t, (start, size) in enumerate(tiles):
            send_codes(half, 1, t)
            ref = part.at[:, 2 * half + other, :, start : start + size]
            rc(ref, ref, ps_s.at[half, t], ps_r.at[half, t], sib).wait_send()

    recv(tgt.at[2 + c], ts_s.at[1], ts_r.at[2 + c])
    go(tgt.at[2 + c], tgt.at[2 + c], tf_s.at[0], tf_r.at[c], sib)
    recv(tgt.at[2 + other], tf_s.at[0], tf_r.at[other])
    lax.fori_loop(0, 4, target_far, 0)

    recv(upart.at[2 * zl + other], us_s.at[0], us_r.at[2 * zl + other])
    for core in range(2):
        recv(upart.at[2 * (1 - zl) + core], us_s.at[1], us_r.at[2 * (1 - zl) + core])
    uvec[...] = (upart[0] + upart[1]) + (upart[2] + upart[3])

    def softmax_rows(z, p):
        def rows_of(i, carry):
            rows = sixteen(i)
            logits = psib[z, p, rows, :] + decode(code_in[z, p, rows, :])
            peak = jnp.max(logits, axis=1, keepdims=True)
            columns = norm_col[z, p, rows, :]
            inverse, along = columns[:, 0:1], columns[:, 1:2]
            u = uvec[...]
            exponent = jnp.exp(logits - peak)
            dlogits = u * inverse - along * logits
            total = jnp.sum(exponent, axis=1, keepdims=True)
            shift = jnp.sum(exponent * dlogits, axis=1, keepdims=True)
            first = jnp.sum(exponent * logits, axis=1, keepdims=True)
            weights = tgt[p, pl.ds(pl.multiple_of(i * 32 + z * 16, 16), 16), :].astype(F32)
            weight_total = jnp.sum(weights, axis=1, keepdims=True)
            weight_first = jnp.sum(weights * logits, axis=1, keepdims=True)
            mean = shift / total
            weighted = exponent * (dlogits - mean)
            second = jnp.sum(weighted * logits, axis=1, keepdims=True) + mean * first
            ef[z, 0, p, rows, :] = exponent.astype(BF16)
            ef[z, 1, p, rows, :] = weighted.astype(BF16)
            st_col[z, p // 2, pl.ds(pl.multiple_of((p % 2) * 64 + i * 16, 16), 16), :] = lanes(
                [peak, total, shift, first, second, weight_total, weight_first]
            )
            return carry

        lax.fori_loop(0, 64 // ROWS, rows_of, 0)

    def softmax(z):
        for half in range(2):
            p = 2 - 2 * half + c
            for t, (start, size) in enumerate(tiles):
                recv(code_in.at[z, p, :, start : start + size], cs_s.at[half, z, t], cs_r.at[half, z, t])
            softmax_rows(z, p)
            go(ef.at[z, :, p], ef.at[z, :, p], cf_s.at[z, half], cf_r.at[z, half], sib)
        mine = pl.ds(pl.multiple_of(c * 64, 64), 64)
        go(st_col.at[z, :, mine, :], st_col.at[z, :, mine, :], cf_s.at[z, 2], cf_r.at[z, 2], sib)
        recv(st_col.at[z, :, pl.ds(pl.multiple_of(other * 64, 64), 64), :], cf_s.at[z, 2], cf_r.at[z, 2])
        for pp in range(2):
            st_in[z, 10, pp] = st_col[z, pp].T[0:8, :]

    def sibling_rows(z):
        for half in range(2):
            recv(ef.at[z, :, 2 - 2 * half + other], cf_s.at[z, half], cf_r.at[z, half])

    def products(z, n):
        cols = pl.ds(pl.multiple_of(n * 512, 512), 512)
        block = head[cols, :]
        got = lax.dot_general(ef[z].reshape(512, width), block, NT, preferred_element_type=F32)
        for p in range(4):
            part[z, p, :, cols] = got[p * 64 : (p + 1) * 64]
            psib[z, p, :, cols] = got[256 + p * 64 : 256 + (p + 1) * 64]

    def merge(a, b):
        peak = jnp.maximum(a[:, 0:1], b[:, 0:1])
        place = lax.broadcasted_iota(jnp.int32, (2, 8, 128), 1)
        scale_a = jnp.where(place < 5, jnp.exp(a[:, 0:1] - peak), 1.0)
        scale_b = jnp.where(place < 5, jnp.exp(b[:, 0:1] - peak), 1.0)
        return jnp.where(place == 0, peak, a * scale_a + b * scale_b)

    def share(z, source, first, step):
        for k in (1, 2, 3):
            slot = first + k - 1
            go(st_in.at[z, source], st_in.at[z, slot], xs_s.at[z, slot], xs_r.at[z, slot], step(k))

    def gather(z, source, first):
        total = st_in[z, source]
        for k in (1, 2, 3):
            slot = first + k - 1
            recv(st_in.at[z, slot], xs_s.at[z, slot], xs_r.at[z, slot])
            total = merge(total, st_in[z, slot])
        return total

    def columns_of(lines, dest):
        sq[...] = jnp.zeros((128, 128), F32)
        for place, line in enumerate(lines):
            sq[place : place + 1, :] = line
        dest[...] = sq[...].T

    def factors(mine, whole):
        factor = jnp.exp(mine[0:1] - whole[0:1])
        return [factor, factor * (mine[2:3] / mine[1:2] - whole[2:3] / whole[1:2])]

    def first_totals(z):
        st_in[z, 11] = gather(z, 10, 0)
        share(z, 11, 6, yn)
        st_in[z, 12] = gather(z, 10, 3)
        for pp in range(2):
            own = st_in[z, 10, pp]
            columns_of(factors(own, st_in[z, 11, pp]) + factors(own, st_in[z, 12, pp]), fin_col.at[pp])
        for p in range(4):
            columns = fin_col[p // 2, (p % 2) * 64 : (p % 2) * 64 + 64, :]
            for kind in range(4):
                wide[kind, p] = jnp.broadcast_to(columns[:, kind : kind + 1], (64, 128))

    def second_totals(z):
        st_in[z, 13] = gather(z, 11, 6)
        go(st_in.at[z, 13], st_in.at[z, 9], xs_s.at[z, 9], xs_r.at[z, 9], flip)
        for pp in range(2):
            both = st_in[z, 13, pp]
            columns_of(factors(st_in[z, 11, pp], both) + factors(st_in[z, 12, pp], both), fin2.at[z, pp])

    def first_stage(z):
        def chunk(n, carry):
            place = z * 4 + n
            for p in range(4):
                for route in range(2):
                    factor, turn = wide[2 * route, p], wide[2 * route + 1, p]
                    for h in range(2):
                        cols = pl.ds(pl.multiple_of(n * 512 + route * 256 + h * 128, 128), 128)
                        value = part[z, p, :, cols]
                        scaled = (factor * value).astype(BF16)
                        weighted = (factor * psib[z, p, :, cols] + turn * value).astype(BF16)
                        for o, rows in enumerate((scaled, weighted)):
                            if route == 1:
                                sb[1, place, h, p, o] = rows
                            else:
                                for k in range(4):
                                    sb[0, place, h, k, o, pl.ds(p * 16, 16), :] = rows[k * 16 : (k + 1) * 16]
            m1.send(place)

            @pl.when(n < 3)
            def _():
                products(z, n + 1)

            @pl.when(n > 0)
            def _():
                m1.relay(place - 1)

            return carry

        lax.fori_loop(0, 4, chunk, 0)

    def second_stage(z):
        def chunk(n, carry):
            place = z * 4 + n
            m1.wait(place)
            for route in range(2):
                for h in range(2):
                    for d in range(4):
                        rows = pl.ds(d * 16, 16)
                        if route == 0:
                            columns = fin2[z, d // 2, pl.ds(pl.multiple_of((d % 2) * 64 + x * 16, 16), 16), :][:, 0:2]
                        else:
                            here = pl.ds(pl.multiple_of((p_mine % 2) * 64 + d * 16, 16), 16)
                            columns = fin2[z, p_mine // 2, here, :][:, 2:4]
                        e_sum = m1.total(route, place, h, 0, rows)
                        f_sum = m1.total(route, place, h, 1, rows)
                        s2[route, place, h, d, 0] = (columns[:, 0:1] * e_sum).astype(BF16)
                        s2[route, place, h, d, 1] = (columns[:, 0:1] * f_sum + columns[:, 1:2] * e_sum).astype(BF16)
            m2.send(place)
            return carry

        lax.fori_loop(0, 4, chunk, 0)

    def last_copy(sent, landed, ssem, rsem, place, n):
        return rc(sent.at[place], landed.at[n], ssem.at[n], rsem.at[n], flip)

    def main_last(z):
        def chunk(n, carry):
            place = z * 4 + n
            m2.wait(place)
            for route in range(2):
                for h in range(2):
                    for o in range(2):
                        value = m2.total(route, place, h, o, pl.ds(0, 16))
                        t2[place, o, :, route * 256 + h * 128 : route * 256 + h * 128 + 128] = value

            @pl.when(zh != z)
            def _():
                s3[place] = t2[place].astype(BF16)
                last_copy(s3, r3, z_s, z_r, place, n).start()

            return carry

        lax.fori_loop(0, 4, chunk, 0)

    def target_second(n, carry):
        g1.wait(n)
        for route in range(2):
            for h in range(2):
                for d in range(4):
                    gs2[route, n, h, d, 0] = g1.total(route, n, h, 0, pl.ds(d * 32, 32)).astype(BF16)
        g2.send(n)
        return carry

    def target_last(n, carry):
        g2.wait(n)
        for route in range(2):
            for h in range(2):
                value = g2.total(route, n, h, 0, pl.ds(0, 32))
                for z in range(2):
                    gt2[n, 0, z, :, route * 256 + h * 128 : route * 256 + h * 128 + 128] = value[z * 16 : (z + 1) * 16]
        gs3[n, 0] = gt2[n, 0, 1 - zh].astype(BF16)
        last_copy(gs3, gr3, gz_s, gz_r, n, n).start()
        return carry

    def relays(reduce, first):
        def one(n, carry):
            reduce.relay(first + n)
            return carry

        lax.fori_loop(0, 4, one, 0)

    softmax(0)
    share(0, 10, 0, xn)
    share(0, 10, 3, yn)
    relays(g1, 0)
    sibling_rows(0)
    products(0, 0)
    first_totals(0)
    first_stage(0)
    lax.fori_loop(0, 4, target_second, 0)
    second_totals(0)
    m1.relay(3)

    softmax(1)
    share(1, 10, 0, xn)
    share(1, 10, 3, yn)
    second_stage(0)
    sibling_rows(1)
    products(1, 0)
    first_totals(1)
    relays(m2, 0)
    first_stage(1)
    relays(g2, 0)
    second_totals(1)
    m1.relay(7)
    main_last(0)
    second_stage(1)
    lax.fori_loop(0, 4, target_last, 0)
    g1.drain()
    m1.drain()
    relays(m2, 4)
    g2.drain()
    for copy in sends:
        copy.wait_send()

    for z in range(2):
        recv(st_in.at[z, 9], xs_s.at[z, 9], xs_r.at[z, 9])
    st_in[zh, 14] = merge(st_in[zh, 13], st_in[zh, 9])
    whole = st_in[zh, 14, p_mine // 2]
    shift = whole[2:3] / whole[1:2]
    mean_logit = whole[3:4] / whole[1:2]
    lines = []
    for slot in (13, 9):
        lines += [line / whole[1:2] for line in factors(st_in[zh, slot, p_mine // 2], whole)]
    weight = 1.0 / whole[5:6]
    lines += [weight, mean_logit - whole[6:7] * weight, whole[4:5] / whole[1:2] - shift * mean_logit]
    columns_of(lines, fin3)

    main_last(1)

    rows = pl.ds(pl.multiple_of(x * 32 + zh * 16, 16), 16)
    norms = norm_col[zh, p_mine, pl.ds(pl.multiple_of(x * 16, 16), 16), :]
    inverse = norms[:, 0:1]
    out_col[...] = norms
    columns = fin3[pl.ds(pl.multiple_of((p_mine % 2) * 64 + x * 16, 16), 16), :]

    def column(place):
        return columns[:, place : place + 1]

    def finish_chunk(n, carry):
        cols = pl.ds(pl.multiple_of(n * 512, 512), 512)
        far = pl.ds(pl.multiple_of(s * depth + n * 512, 512), 512)
        last_copy(gs3, gr3, gz_s, gz_r, n, n).wait_recv()
        last_copy(s3, r3, z_s, z_r, n, n).wait_recv()
        inputs = hid[p_mine, rows, cols].astype(F32) + steer[:, far]
        place = zh * 4 + n
        e_own, e_far = t2[place, 0], r3[n, 0].astype(F32)
        f_own, f_far = t2[place, 1], r3[n, 1].astype(F32)
        targets = gt2[n, 0, zh] + gr3[n, 0].astype(F32)
        grad = column(0) * e_own + column(2) * e_far - column(4) * targets
        ggn = column(0) * f_own + column(1) * e_own + column(2) * f_far + column(3) * e_far
        for o, back in enumerate((grad, ggn)):
            slope = column(5 + o) * inverse * (1.0 / full)
            out[o, :, cols] = gain[:, far] * back - inputs * slope
        return carry

    lax.fori_loop(0, 4, finish_chunk, 0)

    m2.drain()
    for n in range(4):
        last_copy(gs3, gr3, gz_s, gz_r, n, n).wait_send()
        last_copy(s3, r3, z_s, z_r, n, n).wait_send()


def body(hidden, steer, tangent, gain, head, target):
    vmem = pltpu.VMEM
    dma = pltpu.SemaphoreType.DMA
    any_spec = pl.BlockSpec(memory_space=pl.ANY)
    vmem_spec = pl.BlockSpec(memory_space=pltpu.VMEM)
    result, columns = pl.pallas_call(
        kernel,
        out_shape=[jax.ShapeDtypeStruct((2, 16, 2048), F32), jax.ShapeDtypeStruct((16, 128), F32)],
        in_specs=[any_spec] * 3 + [vmem_spec] * 3,
        out_specs=[vmem_spec] * 2,
        scratch_shapes=[
            vmem((128, 8192), BF16),
            vmem((4, 128, 2048), BF16),
            vmem((4, 8, 128), F32),
            vmem((128, 128), F32),
            vmem((2048, 2432), BF16),
            vmem((272, 2048), BF16),
            vmem((256, 2048), BF16),
            vmem((4, 1, 2432), F32),
            vmem((1, 2432), F32),
            vmem((2, 4, 64, 2432), F32),
            vmem((2, 4, 64, 2432), F32),
            vmem((2, 2, 64, 2432), BF16),
            vmem((2, 4, 64, 2432), BF16),
            vmem((4, 128, 2432), BF16),
            vmem((2, 2, 4, 64, 2432), BF16),
            vmem((2, 4, 64, 128), F32),
            vmem((2, 2, 128, 128), F32),
            vmem((2, 15, 2, 8, 128), F32),
            vmem((2, 128, 128), F32),
            vmem((4, 4, 64, 128), F32),
            vmem((2, 2, 128, 128), F32),
            vmem((128, 128), F32),
            vmem((2, 8, 2, 4, 2, 64, 128), BF16),
            vmem((2, 8, 2, 3, 2, 64, 128), BF16),
            vmem((2, 8, 2, 4, 2, 16, 128), BF16),
            vmem((2, 8, 2, 3, 2, 16, 128), BF16),
            vmem((8, 2, 16, 512), F32),
            vmem((8, 2, 16, 512), BF16),
            vmem((4, 2, 16, 512), BF16),
            vmem((2, 4, 2, 4, 1, 128, 128), BF16),
            vmem((2, 4, 2, 3, 1, 128, 128), BF16),
            vmem((2, 4, 2, 4, 1, 32, 128), BF16),
            vmem((2, 4, 2, 3, 1, 32, 128), BF16),
            vmem((4, 1, 2, 16, 512), F32),
            vmem((4, 1, 16, 512), BF16),
            vmem((4, 1, 16, 512), BF16),
            dma((4,)),
            dma((1,)), dma((4,)),
            dma((2, 2)), dma((2, 2)),
            dma((2, 2, 4)), dma((2, 2, 4)),
            dma((3,)), dma((4,)),
            dma((3,)), dma((4,)),
            dma((2,)), dma((4,)),
            dma((1,)), dma((2,)),
            dma((2, 5)), dma((2, 5)),
            dma((2, 2, 5)), dma((2, 2, 5)),
            dma((2, 3)), dma((2, 3)),
            dma((2, 10)), dma((2, 10)),
            dma((1,)), dma((8, 2)),
            dma((1,)), dma((8, 2)),
            dma((4,)), dma((4,)),
            dma((1,)), dma((4, 2)),
            dma((1,)), dma((4, 2)),
            dma((4,)), dma((4,)),
        ],
        compiler_params=pltpu.CompilerParams(
            collective_id=0, has_side_effects=True, vmem_limit_bytes=64 * 1024 * 1024 - 65536
        ),
    )(hidden, head, target, steer.reshape(1, -1), tangent.reshape(1, -1), gain.reshape(1, -1))
    inverse = columns[:, 0:1]
    return result[0] * inverse, result[1] * inverse


def solution(mesh):
    return jax.shard_map(
        body,
        mesh=mesh,
        in_specs=(P("seq", None), P(), P(), P(), P("seq", "vocab"), P("seq", "vocab")),
        out_specs=(P("vocab", "seq"), P("vocab", "seq")),
        check_vma=False,
    )
```

time: 845 us -> 96 us (0.11)
  waiting for transfers between devices: 567 us -> 0 us
  blocking collectives: 196 us -> 0 us
  Pallas kernels: 0 us -> 92.6 us
  matrix products: 35.5 us -> 0 us
  other arithmetic: 20.7 us -> 1.76 us
  between operations: 13.9 us -> 0.64 us
    psum x1 -> x0, waiting for transfers between devices: 402 us -> none  [body(): lax.psum(jnp.concatenate([first_part, second_part], axis=1), 'vocab')]
    psum x3 -> x0, blocking collectives: 100 us -> none  [the longest x1 88.9 us: body(): lax.psum((jnp.sum(exponent, axis=1), jnp.sum(exponent * dlogits, axis=1),...]
    pmax x1 -> x0, blocking collectives: 96 us -> none  [body(): row_peak = lax.pmax(local_peak, 'vocab')]
    reduce_scatter x1 -> x0, waiting for transfers between devices: 93 us -> none  [body(): lax.psum_scatter(jnp.concatenate([jnp.dot(normed, head, preferred_element...]
    pallas_call x0 -> x1, Pallas kernels: none -> 92.6 us  [body(): pl.pallas_call(kernel, out_shape=[jax.ShapeDtypeStruct((2, 16, 2048), F32...]
    all_gather x1 -> x0, waiting for transfers between devices: 49 us -> none  [body(): gathered = lax.all_gather(cotangent, 'seq', axis=0, tiled=True)]
    dot_general x4 -> x0, matrix products: 35.5 us -> none  [the longest x1 10.6 us: body(): jnp.dot(normed, head, preferred_element_type=jnp.float32)]
    all_to_all x1 -> x0, waiting for transfers between devices: 23.5 us -> none  [body(): lax.all_to_all(hidden, 'seq', split_axis=1, concat_axis=0, tiled=True)]
  transfers between devices with their start and end apart: 4 -> 0, of which waited for: 4 -> 0; matrix products, arithmetic and copies ran while one was open for 0% -> 0% of each run, Pallas kernels for 0% -> 0%
where the time goes in v2:
time: 96 us; the launch traced here: 95.8 us
  Pallas kernels  92.6 us (96%)
  other arithmetic  1.76 us (2%)
    pallas_call x1, Pallas kernels, body(): pl.pallas_call(kernel, out_shape=[jax.ShapeDtypeStruct((2, 16, 2048), F32...  92.6 us

profile of v2, /device:TPU:0, one launch (start us, length us, event | category | flops | bytes accessed | tf_op | source)
XLA Modules:
  0.0 95.8 jit_solution(15325669693956688783)
XLA Ops:
  0.6 92.6 %shard_map.77 = (f32[2,16,2048]{2,1,0:T(8,128)}, f32[16,128]{1,0:T(8,128)}) custom-call(bf16[128,8192]{1,0:T(8,128)(2,1)} %hidden.1, bf16[2048,2432]{1,0:T(8,128)(2,1)} %head_hbm.1, bf16[128,2432]{1,0:T(8,128)(2,1)} %target.1, f32[1,8192]{1,0:T(1,128)} %bitcast.7, f32[1,8192]{1,0:T(1,128)} %bitcast.8, f32[1,8192]{1,0:T(1,128)} %bitcast.9), custom_call_target="tpu_custom_call" | custom-call | tf_op jit(solution)/shard_map/pallas_call | solution.py:665
  93.2 0.8 slice_reduce_fusion
  94.0 1.8 %bitcast_multiply_fusion = (f32[16,2048]{1,0:T(8,128)}, f32[16,2048]{1,0:T(8,128)}) fusion(f32[2,16,2048]{2,1,0:T(8,128)} %get-tuple-element.4, f32[16]{0:T(128)S(1)} %slice_reduce_fusion), kind=kLoop, calls=%fused_computation | loop fusion | flops 65536 | bytes 524352 | tf_op jit(solution)/shard_map/mul | solution.py:731

commit v3 on v2

--- a/solution.py
+++ b/solution.py
@@ -98,7 +98,7 @@
 
 def kernel(
     hidden, head_hbm, target, steer, tangent, gain,
-    out, out_col,
+    out, out_sub,
     hfull, hid, stats_in, sq, head, nrm_loc, nrm_rem, upart, uvec, part, psib, code_out, code_in, tgt,
     ef, norm_col, st_col, st_in, fin_col, wide, fin2, fin3,
     sb, r1, s2, r2, t2, s3, r3, gsb, gr1, gs2, gr2, gt2, gs3, gr3,
@@ -171,12 +171,38 @@
     peers = [sib, pair(0), pair(1), zo(0), zo(1), flip] + [xn(k) for k in (1, 2, 3)] + [yn(k) for k in (1, 2, 3)]
     for peer in peers:
         pl.semaphore_signal(barrier, inc=1, device_id=peer, device_id_type=MESH)
+    steer_part = steer[:, my_cols]
+    gain_part = gain[:, my_cols]
+    product = gain_part * tangent[:, my_cols]
+    high = product.astype(BF16).astype(F32)
+    row = lax.broadcasted_iota(jnp.int32, (16, depth), 0)
+    nrm_loc[256:272, :] = jnp.where(row == 0, high, jnp.where(row == 1, product - high, 0.0)).astype(BF16)
+
+    load_hfull.wait()
+
+    def sums(i, carry):
+        rows = sixteen(i)
+        squares = jnp.zeros((ROWS, 1), F32)
+        dots = jnp.zeros((ROWS, 1), F32)
+        for q in range(8):
+            cols = pl.ds(q * 1024, 1024)
+            inputs = hfull[rows, cols].astype(F32) + steer[:, cols]
+            squares += jnp.sum(inputs * inputs, axis=1, keepdims=True)
+            dots += jnp.sum(inputs * tangent[:, cols], axis=1, keepdims=True)
+        sq[rows, :] = lanes([squares, dots])
+        return carry
+
+    lax.fori_loop(0, 128 // ROWS, sums, 0)
+    stats_in[c] = sq[...].T[0:8, :]
     pl.semaphore_wait(barrier, len(peers))
 
     def piece(half, k):
         place = ((x if half == 0 else y) + k) % 4
         return pl.ds(pl.multiple_of(half * 64 + place * 16, 16), 16)
 
+    for place, dev in enumerate((sib, zo(0), zo(1))):
+        slot = c if place == 0 else 2 + c
+        go(stats_in.at[c], stats_in.at[slot], ss_s.at[place], ss_r.at[slot], dev)
     go(hidden.at[:, cols_of(2 * zl + 1 - c)], hid.at[c], hs_s.at[0], hs_r.at[c], sib)
     for core in range(2):
         for half in range(2):
@@ -190,26 +216,6 @@
     go(tgt.at[c], tgt.at[c], ts_s.at[0], ts_r.at[c], sib)
     load_head.start()
 
-    load_hfull.wait()
-
-    def sums(i, carry):
-        rows = sixteen(i)
-        squares = jnp.zeros((ROWS, 1), F32)
-        dots = jnp.zeros((ROWS, 1), F32)
-        for q in range(8):
-            cols = pl.ds(q * 1024, 1024)
-            inputs = hfull[rows, cols].astype(F32) + steer[:, cols]
-            squares += jnp.sum(inputs * inputs, axis=1, keepdims=True)
-            dots += jnp.sum(inputs * tangent[:, cols], axis=1, keepdims=True)
-        sq[rows, :] = lanes([squares, dots])
-        return carry
-
-    lax.fori_loop(0, 128 // ROWS, sums, 0)
-    stats_in[c] = sq[...].T[0:8, :]
-    for place, dev in enumerate((sib, zo(0), zo(1))):
-        slot = c if place == 0 else 2 + c
-        go(stats_in.at[c], stats_in.at[slot], ss_s.at[place], ss_r.at[slot], dev)
-
     def hop(half, k):
         return xn(k) if half == 0 else yn(k)
 
@@ -236,8 +242,6 @@
                 ref = hid.at[2 + core, piece(half, 2), way * 1024 : (way + 1) * 1024]
                 recv(ref, hr_s.at[core, half, 2 + way], hr_r.at[core, half, 2 + way])
 
-    steer_part = steer[:, my_cols]
-    gain_part = gain[:, my_cols]
 
     def norm_block(p, dest, base):
         sq[...] = jnp.zeros((128, 128), F32)
@@ -256,27 +260,21 @@
 
         lax.fori_loop(0, 128 // ROWS, rows_of, 0)
 
-    product = gain_part * tangent[:, my_cols]
-    high = product.astype(BF16).astype(F32)
-    row = lax.broadcasted_iota(jnp.int32, (16, depth), 0)
-    nrm_loc[256:272, :] = jnp.where(row == 0, high, jnp.where(row == 1, product - high, 0.0)).astype(BF16)
-
     load_own.wait()
     recv(hid.at[other], hs_s.at[0], hs_r.at[other])
     recv(stats_in.at[other], ss_s.at[0], ss_r.at[other])
     norm_block(0, nrm_loc, 0)
     norm_block(1, nrm_loc, 64)
-    ring_start()
     load_head.wait()
 
     tiles = [(0, 512), (512, 512), (1024, 512), (1536, 512), (2048, 384)]
 
     def send_codes(half, z, t):
         cols = slice(tiles[t][0], tiles[t][0] + tiles[t][1])
-        go(
+        rc(
             code_out.at[half, z, :, cols], code_in.at[z, 2 - 2 * half + c, :, cols],
-            cs_s.at[half, z, t], cs_r.at[half, z, t], pair(c),
-        )
+            cs_s.at[0], cs_r.at[half, z], pair(c),
+        ).start()
 
     def forward(half):
         p0 = 2 * half
@@ -311,6 +309,8 @@
                 part.at[:, p0 + other, :, cols], psib.at[:, p0 + other, :, cols],
                 ps_s.at[half, t], ps_r.at[half, t], sib,
             ).start()
+            if half == 0 and t == 2:
+                ring_start()
             if t:
                 finish(t - 1)
         finish(len(tiles) - 1)
@@ -346,9 +346,12 @@
     forward(0)
     for place, dev in enumerate((sib, pair(0), pair(1))):
         go(upart.at[s], upart.at[s], us_s.at[place], us_r.at[s], dev)
+    recv(tgt.at[other], ts_s.at[0], ts_r.at[other])
+    lax.fori_loop(0, 2, target_near, 0)
     ring_relay()
-    recv(tgt.at[other], ts_s.at[0], ts_r.at[other])
-    lax.fori_loop(0, 4, target_near, 0)
+    lax.fori_loop(2, 4, target_near, 0)
+    recv(tgt.at[2 + c], ts_s.at[1], ts_r.at[2 + c])
+    go(tgt.at[2 + c], tgt.at[2 + c], tf_s.at[0], tf_r.at[c], sib)
     for core in range(2):
         ring_end(core)
         recv(stats_in.at[2 + core], ss_s.at[1], ss_r.at[2 + core])
@@ -360,8 +363,6 @@
             ref = part.at[:, 2 * half + other, :, start : start + size]
             rc(ref, ref, ps_s.at[half, t], ps_r.at[half, t], sib).wait_send()
 
-    recv(tgt.at[2 + c], ts_s.at[1], ts_r.at[2 + c])
-    go(tgt.at[2 + c], tgt.at[2 + c], tf_s.at[0], tf_r.at[c], sib)
     recv(tgt.at[2 + other], tf_s.at[0], tf_r.at[other])
     lax.fori_loop(0, 4, target_far, 0)
 
@@ -401,10 +402,11 @@
     def softmax(z):
         for half in range(2):
             p = 2 - 2 * half + c
-            for t, (start, size) in enumerate(tiles):
-                recv(code_in.at[z, p, :, start : start + size], cs_s.at[half, z, t], cs_r.at[half, z, t])
+            recv(code_in.at[z, p], cs_s.at[0], cs_r.at[half, z])
             softmax_rows(z, p)
             go(ef.at[z, :, p], ef.at[z, :, p], cf_s.at[z, half], cf_r.at[z, half], sib)
+            if z == 1 and half == 0:
+                m1.relay(3)
         mine = pl.ds(pl.multiple_of(c * 64, 64), 64)
         go(st_col.at[z, :, mine, :], st_col.at[z, :, mine, :], cf_s.at[z, 2], cf_r.at[z, 2], sib)
         recv(st_col.at[z, :, pl.ds(pl.multiple_of(other * 64, 64), 64), :], cf_s.at[z, 2], cf_r.at[z, 2])
@@ -433,14 +435,13 @@
     def share(z, source, first, step):
         for k in (1, 2, 3):
             slot = first + k - 1
-            go(st_in.at[z, source], st_in.at[z, slot], xs_s.at[z, slot], xs_r.at[z, slot], step(k))
+            rc(st_in.at[z, source], st_in.at[z, slot], xs_s.at[0], xs_r.at[z, first // 3], step(k)).start()
 
     def gather(z, source, first):
+        recv(st_in.at[z, first : first + 3], xs_s.at[0], xs_r.at[z, first // 3])
         total = st_in[z, source]
-        for k in (1, 2, 3):
-            slot = first + k - 1
-            recv(st_in.at[z, slot], xs_s.at[z, slot], xs_r.at[z, slot])
-            total = merge(total, st_in[z, slot])
+        for k in range(3):
+            total = merge(total, st_in[z, first + k])
         return total
 
     def columns_of(lines, dest):
@@ -467,7 +468,7 @@
 
     def second_totals(z):
         st_in[z, 13] = gather(z, 11, 6)
-        go(st_in.at[z, 13], st_in.at[z, 9], xs_s.at[z, 9], xs_r.at[z, 9], flip)
+        rc(st_in.at[z, 13], st_in.at[z, 9], xs_s.at[0], xs_r.at[z, 3], flip).start()
         for pp in range(2):
             both = st_in[z, 13, pp]
             columns_of(factors(st_in[z, 11, pp], both) + factors(st_in[z, 12, pp], both), fin2.at[z, pp])
@@ -491,13 +492,13 @@
                                     sb[0, place, h, k, o, pl.ds(p * 16, 16), :] = rows[k * 16 : (k + 1) * 16]
             m1.send(place)
 
-            @pl.when(n < 3)
+            @pl.when(n < 2)
             def _():
-                products(z, n + 1)
-
-            @pl.when(n > 0)
+                products(z, n + 2)
+
+            @pl.when(n > 1)
             def _():
-                m1.relay(place - 1)
+                m1.relay(place - 2)
 
             return carry
 
@@ -580,11 +581,12 @@
     relays(g1, 0)
     sibling_rows(0)
     products(0, 0)
+    products(0, 1)
     first_totals(0)
     first_stage(0)
+    m1.relay(2)
     lax.fori_loop(0, 4, target_second, 0)
     second_totals(0)
-    m1.relay(3)
 
     softmax(1)
     share(1, 10, 0, xn)
@@ -592,9 +594,11 @@
     second_stage(0)
     sibling_rows(1)
     products(1, 0)
+    products(1, 1)
     first_totals(1)
     relays(m2, 0)
     first_stage(1)
+    m1.relay(6)
     relays(g2, 0)
     second_totals(1)
     m1.relay(7)
@@ -609,7 +613,7 @@
         copy.wait_send()
 
     for z in range(2):
-        recv(st_in.at[z, 9], xs_s.at[z, 9], xs_r.at[z, 9])
+        recv(st_in.at[z, 9], xs_s.at[0], xs_r.at[z, 3])
     st_in[zh, 14] = merge(st_in[zh, 13], st_in[zh, 9])
     whole = st_in[zh, 14, p_mine // 2]
     shift = whole[2:3] / whole[1:2]
@@ -626,7 +630,6 @@
     rows = pl.ds(pl.multiple_of(x * 32 + zh * 16, 16), 16)
     norms = norm_col[zh, p_mine, pl.ds(pl.multiple_of(x * 16, 16), 16), :]
     inverse = norms[:, 0:1]
-    out_col[...] = norms
     columns = fin3[pl.ds(pl.multiple_of((p_mine % 2) * 64 + x * 16, 16), 16), :]
 
     def column(place):
@@ -646,12 +649,15 @@
         ggn = column(0) * f_own + column(1) * e_own + column(2) * f_far + column(3) * e_far
         for o, back in enumerate((grad, ggn)):
             slope = column(5 + o) * inverse * (1.0 / full)
-            out[o, :, cols] = gain[:, far] * back - inputs * slope
+            out[o, :, cols] = gain[:, far] * back * inverse
+            out_sub[o, :, cols] = inputs * slope * inverse
         return carry
 
     lax.fori_loop(0, 4, finish_chunk, 0)
 
     m2.drain()
+    rc(st_in.at[:, 0:10], st_in.at[:, 0:10], xs_s.at[0], xs_r.at[0, 0], sib).wait_send()
+    rc(code_out, code_out, cs_s.at[0], cs_r.at[0, 0], sib).wait_send()
     for n in range(4):
         last_copy(gs3, gr3, gz_s, gz_r, n, n).wait_send()
         last_copy(s3, r3, z_s, z_r, n, n).wait_send()
@@ -662,9 +668,9 @@
     dma = pltpu.SemaphoreType.DMA
     any_spec = pl.BlockSpec(memory_space=pl.ANY)
     vmem_spec = pl.BlockSpec(memory_space=pltpu.VMEM)
-    result, columns = pl.pallas_call(
+    result, less = pl.pallas_call(
         kernel,
-        out_shape=[jax.ShapeDtypeStruct((2, 16, 2048), F32), jax.ShapeDtypeStruct((16, 128), F32)],
+        out_shape=[jax.ShapeDtypeStruct((2, 16, 2048), F32)] * 2,
         in_specs=[any_spec] * 3 + [vmem_spec] * 3,
         out_specs=[vmem_spec] * 2,
         scratch_shapes=[
@@ -713,9 +719,9 @@
             dma((2,)), dma((4,)),
             dma((1,)), dma((2,)),
             dma((2, 5)), dma((2, 5)),
-            dma((2, 2, 5)), dma((2, 2, 5)),
+            dma((1,)), dma((2, 2)),
             dma((2, 3)), dma((2, 3)),
-            dma((2, 10)), dma((2, 10)),
+            dma((1,)), dma((2, 4)),
             dma((1,)), dma((8, 2)),
             dma((1,)), dma((8, 2)),
             dma((4,)), dma((4,)),
@@ -727,8 +733,7 @@
             collective_id=0, has_side_effects=True, vmem_limit_bytes=64 * 1024 * 1024 - 65536
         ),
     )(hidden, head, target, steer.reshape(1, -1), tangent.reshape(1, -1), gain.reshape(1, -1))
-    inverse = columns[:, 0:1]
-    return result[0] * inverse, result[1] * inverse
+    return result[0] - less[0], result[1] - less[1]
 
 
 def solution(mesh):

time: 96 us -> 91.5 us (0.953)
  Pallas kernels: 92.6 us -> 88.9 us
    pallas_call x1, Pallas kernels: 92.6 us -> 88.9 us  [body(): pl.pallas_call(kernel, out_shape=[jax.ShapeDtypeStruct((2, 16, 2048), F32...]
    sub x0 -> x1, other arithmetic: none -> 1.82 us  [body(): return (result[0] - less[0], result[1] - less[1])]
    mul x1 -> x0, other arithmetic: 1.76 us -> none  [body(): return (result[0] * inverse, result[1] * inverse)]
where the time goes in v3:
time: 91.5 us; the launch traced here: 91.3 us
  Pallas kernels  88.9 us (97%)
  other arithmetic  1.82 us (2%)
    pallas_call x1, Pallas kernels, body(): pl.pallas_call(kernel, out_shape=[jax.ShapeDtypeStruct((2, 16, 2048), F32...  88.9 us

profile of v3, /device:TPU:0, one launch (start us, length us, event | category | flops | bytes accessed | tf_op | source)
XLA Modules:
  0.0 91.3 jit_solution(8274730973440031378)
XLA Ops:
  0.6 88.9 %shard_map.77 = (f32[2,16,2048]{2,1,0:T(8,128)}, f32[2,16,2048]{2,1,0:T(8,128)}) custom-call(bf16[128,8192]{1,0:T(8,128)(2,1)} %hidden.1, bf16[2048,2432]{1,0:T(8,128)(2,1)} %head_hbm.1, bf16[128,2432]{1,0:T(8,128)(2,1)} %target.1, f32[1,8192]{1,0:T(1,128)} %bitcast.7, f32[1,8192]{1,0:T(1,128)} %bitcast.8, f32[1,8192]{1,0:T(1,128)} %bitcast.9), custom_call_target="tpu_custom_call" | custom-call | tf_op jit(solution)/shard_map/pallas_call | solution.py:671
  89.5 1.8 %subtract_bitcast_fusion = (f32[16,2048]{1,0:T(8,128)}, f32[16,2048]{1,0:T(8,128)}) fusion(f32[2,16,2048]{2,1,0:T(8,128)} %get-tuple-element.5, f32[2,16,2048]{2,1,0:T(8,128)} %get-tuple-element.4), kind=kLoop, calls=%fused_computation | loop fusion | flops 65536 | bytes 786432 | tf_op jit(solution)/shard_map/sub | solution.py:736
